TPU v7x, 256 devices: a whole 4x4x8 slice. The times are simulated.
256 devices in a mesh: ma: 32 (over z, x_lo, core), bl: 8 (over y, x_hi).
Axes of the slice: x: 4 (x_hi: 2, x_lo: 2; x = x_hi * 2 + x_lo), y: 4, z: 8, core: 2. Of those that a mesh axis runs over, the one named last changes fastest.
Arguments:
- visibilities: bfloat16 [2, 16640, 8192], P(None, 'bl', 'ma'), may hold values from -6 to 6
- beam_blocks: bfloat16 [32, 2, 16640, 1000], P('ma', None, 'bl'), may hold values from -0.0625 to 0.0625
- feed_pairs: int32 [16640, 2], P('bl'), may hold values from 0 to 1023
- feed_gains: float32 [2, 1024], replicated, may hold values from -1.5 to 1.5
- m_order: int32 [32], replicated, may hold values from 0 to 31, each once
Outputs:
- sky_modes: float32 [2, 32, 1000], P(None, 'ma', 'bl')
All inputs are finite; a program needn't handle non-finite values.
Results may differ from a plain program's by a relative error of at most 0.0049.
Values may be sent and summed in bfloat16 or wider, within the bound.
No kernel may reach another device: no remote copies, remote signals or barrier semaphores. Data moves between devices by JAX's collectives and lax.ppermute only.
A program may use at most 64 MiB of HBM per device.

v0:
```python
import jax
import jax.numpy as jnp
from jax import lax
from jax.sharding import PartitionSpec as P

NT = 8192


def dft_weights(time_index, m_values):
    wrapped = jnp.mod(time_index[:, None] * m_values[None, :], NT).astype(jnp.float32)
    phases = wrapped * (2.0 * jnp.pi / NT)
    scale = 1.0 / jnp.sqrt(jnp.float32(NT))
    cos_part = (jnp.cos(phases) * scale).astype(jnp.bfloat16)
    sin_part = (jnp.sin(phases) * scale).astype(jnp.bfloat16)
    upper = jnp.concatenate([cos_part, -sin_part], axis=1)
    lower = jnp.concatenate([sin_part, cos_part], axis=1)
    return jnp.concatenate([upper, lower], axis=0)


def transform(visible, weights, count):
    stacked_in = jnp.concatenate([visible[0], visible[1]], axis=1)
    flat = jnp.dot(stacked_in, weights, preferred_element_type=jnp.float32)
    return jnp.stack([flat[:, :count], flat[:, count:]])


def per_device(visibilities, beam_blocks, feed_pairs, feed_gains, m_order):
    count = m_order.shape[0]
    m_values = m_order - count // 2
    turned = lax.all_to_all(visibilities, "ma", split_axis=1, concat_axis=2, tiled=True)
    time_index = jnp.arange(NT, dtype=jnp.int32)
    weights = dft_weights(time_index, m_values)
    spectra_all = transform(turned, weights, count).astype(jnp.bfloat16)
    owned = lax.all_to_all(spectra_all, "ma", split_axis=2, concat_axis=1, tiled=True)
    local_rows = feed_pairs.shape[0]
    feed_count = feed_gains.shape[1]
    both_feeds = jnp.concatenate([feed_pairs[:, 0], feed_pairs[:, 1]], axis=0)
    feed_iota = jnp.arange(feed_count, dtype=jnp.int32)
    one_hot = (both_feeds[:, None] == feed_iota[None, :]).astype(jnp.float32)
    picked = jnp.dot(
        one_hot,
        jnp.transpose(feed_gains),
        precision=lax.Precision.HIGHEST,
        preferred_element_type=jnp.float32,
    )
    a_re = picked[:local_rows, 0]
    a_im = picked[:local_rows, 1]
    b_re = picked[local_rows:, 0]
    b_im = picked[local_rows:, 1]
    factor_re = (a_re * b_re + a_im * b_im)[:, None]
    factor_im = (a_im * b_re - a_re * b_im)[:, None]
    spec_re = owned[0].astype(jnp.float32)
    spec_im = owned[1].astype(jnp.float32)
    weighted_re = (spec_re * factor_re - spec_im * factor_im).astype(jnp.bfloat16)
    weighted_im = (spec_re * factor_im + spec_im * factor_re).astype(jnp.bfloat16)
    row_real = jnp.concatenate([weighted_re, weighted_im], axis=0)
    row_imag = jnp.concatenate([weighted_im, -weighted_re], axis=0)
    vectors = jnp.transpose(jnp.stack([row_real, row_imag]), (2, 0, 1))
    local_modes = beam_blocks.shape[0]
    block_rows = beam_blocks.shape[2]
    width = beam_blocks.shape[3]
    flat_blocks = beam_blocks.reshape(local_modes, 2 * block_rows, width)
    partial_value = jnp.einsum(
        "mkc,mcl->kml", vectors, flat_blocks, preferred_element_type=jnp.float32
    )
    totals = lax.psum(partial_value, "bl")
    share_width = width // lax.axis_size("bl")
    result = lax.dynamic_slice_in_dim(totals, lax.axis_index("bl") * share_width, share_width, 2)
    return result


def solution(mesh):
    return jax.shard_map(
        per_device,
        mesh=mesh,
        in_specs=(P(None, "bl", "ma"), P("ma", None, "bl", None), P("bl", None), P(), P()),
        out_specs=P(None, "ma", "bl"),
        check_vma=False,
    )
```

profile of v0, /device:TPU:32, one launch (start us, length us, event | category | flops | bytes accessed | tf_op | source)
XLA Modules:
  0.0 125.1 jit_solution(16303524143769065953)
XLA Ops:
  0.0 0.0 copy-start
  0.0 14.5 %copy.16 = bf16[2,2080,256]{2,0,1:T(2,128)(2,1)} copy(bf16[2,2080,256]{2,1,0:T(8,128)(2,1)} %param.5) | data formatting | bytes 4259840 | tf_op args[0]
  14.5 9.8 %all-to-all-start = ((bf16[2,2080,256]{2,0,1:T(2,128)(2,1)}), bf16[2,2080,256]{2,0,1:T(2,128)(2,1)S(1)}, u32[]{:S(2)}, u32[]{:S(2)}) async-start(bf16[2,2080,256]{2,0,1:T(2,128)(2,1)} %copy.16), calls=%async_computation | async-start | bytes 4259840 | tf_op jit(solution)/shard_map/all_to_all | solution.py:29
  24.3 0.0 copy-done.2
  24.3 0.1 pad_add_fusion
  24.4 0.0 copy-done.3
  24.4 4.2 %fusion.24 = bf16[8192,32]{0,1:T(8,128)(2,1)S(1)} fusion(s32[32]{0:T(128)S(1)} %broadcast_add_fusion), kind=kLoop, calls=%fused_computation.29 | loop fusion | flops 4980736 | bytes 524416 | tf_op jit(solution)/shard_map/neg | solution.py:15
  28.7 5.2 %multiply_convert_fusion = (bf16[8192,32]{0,1:T(8,128)(2,1)S(1)}, bf16[8192,32]{0,1:T(8,128)(2,1)}) fusion(s32[32]{0:T(128)S(1)} %broadcast_add_fusion), kind=kLoop, calls=%fused_computation.24 | loop fusion | flops 4718592 | bytes 1048704 | tf_op jit(solution)/shard_map/convert_element_type | solution.py:14
  33.9 41.6 %all-to-all-done = bf16[2,2080,256]{2,0,1:T(2,128)(2,1)S(1)} async-done(((bf16[2,2080,256]{2,0,1:T(2,128)(2,1)}), bf16[2,2080,256]{2,0,1:T(2,128)(2,1)S(1)}, u32[]{:S(2)}, u32[]{:S(2)}) %all-to-all-start) | async-done | bytes 2129952 | tf_op jit(solution)/shard_map/all_to_all | solution.py:29
  75.5 3.0 %fusion.31 = (bf16[1,65,32,256]{3,0,1,2:T(2,128)(2,1)S(1)}, bf16[1,65,32,256]{3,0,1,2:T(2,128)(2,1)S(1)}) fusion(bf16[2,65,32,256]{3,0,1,2:T(2,128)(2,1)S(1)} %bitcast.38), kind=kLoop, calls=%fused_computation.53 | loop fusion | bytes 4259840 | tf_op jit(solution)/shard_map/slice | solution.py:21
  78.5 0.6 copy_bitcast_fusion
  79.1 0.1 pad.16
  79.2 0.7 copy.22
  80.0 0.0 copy-start.1
  80.0 0.1 pad.17
  80.1 0.7 copy.23
  80.8 0.2 copy-done.1
  81.0 0.9 fusion.13
  81.9 0.6 copy.19
  82.6 4.4 %all-to-all-start.1 = ((bf16[2,65,32]{1,0,2:T(2,128)(2,1)}), bf16[2,65,32]{1,0,2:T(2,128)(2,1)S(1)}, u32[]{:S(2)}, u32[]{:S(2)}) async-start(bf16[2,65,32]{1,0,2:T(2,128)(2,1)} %copy.19), calls=%async_computation.1 | async-start | bytes 32768 | tf_op jit(solution)/shard_map/all_to_all | solution.py:33
  87.0 0.0 copy-done
  87.0 7.6 %fusion = f32[4160,2]{0,1:T(2,128)S(1)} fusion(f32[2,1024]{1,0:T(2,128)S(1)} %copy-done, s32[4160]{0:T(1024)S(1)} %pad_add_fusion), kind=kOutput, calls=%fused_computation.1 | convolution fusion | flops 106496000 | bytes 58112 | tf_op jit(solution)/shard_map/dot_general | solution.py:39
  94.6 0.0 all-to-all-done.1
  94.6 0.1 fusion.28
  94.7 0.1 reshape.63
  94.8 0.1 reshape.64
  94.9 0.1 add_convert_fusion
  95.1 0.1 maximum_bitcast_fusion
  95.2 0.1 pad_maximum_fusion
  95.2 4.6 %convolution_bitcast_fusion = f32[2,1,1000]{2,0,1:T(2,128)S(1)} fusion(bf16[4160,1000]{1,0:T(8,128)(2,1)} %bitcast.37, bf16[2,4160,1]{1,2,0:T(2,128)(2,1)S(1)} %pad_maximum_fusion), kind=kOutput, calls=%fused_computation.18 | convolution fusion | flops 16640000 | bytes 8344640 | tf_op jit(solution)/shard_map/mkc,mcl->kml/dot_general | solution.py:62
  99.9 24.6 %psum.7 = f32[2,1,1000]{2,0,1:T(2,128)S(1)} all-reduce(f32[2,1,1000]{2,0,1:T(2,128)S(1)} %convolution_bitcast_fusion), channel_id=1, replica_groups=mesh['ma'=32,'bl'=8] {'bl'}, use_global_device_ids=true, to_apply=%region_0.1 | all-reduce | flops 2000 | bytes 16000 | tf_op jit(solution)/shard_map/psum | solution.py:65
  124.4 0.6 constant_dynamic-slice_fusion
  (7 shorter events, 0.1 us)
Async XLA Ops:
  0.0 87.0 %copy-start = (f32[2,1024]{1,0:T(2,128)S(1)}, f32[2,1024]{1,0:T(2,128)}, u32[]{:S(2)}) copy-start(f32[2,1024]{1,0:T(2,128)} %param.8) | copy-start | bytes 24580
  14.5 9.8 %copy-start.2 = (s32[2080,2]{0,1:T(2,128)S(1)}, s32[2080,2]{0,1:T(2,128)}, u32[]{:S(2)}) copy-start(s32[2080,2]{0,1:T(2,128)} %param.7) | copy-start | bytes 49924
  14.5 9.9 %copy-start.3 = (s32[32]{0:T(128)S(1)}, s32[32]{0:T(128)}, u32[]{:S(2)}) copy-start(s32[32]{0:T(128)} %param.9) | copy-start | bytes 388
  14.5 61.0 %all-to-all-start = ((bf16[2,2080,256]{2,0,1:T(2,128)(2,1)}), bf16[2,2080,256]{2,0,1:T(2,128)(2,1)S(1)}, u32[]{:S(2)}, u32[]{:S(2)}) async-start(bf16[2,2080,256]{2,0,1:T(2,128)(2,1)} %copy.16), calls=%async_computation | async-start | bytes 4259840 | tf_op jit(solution)/shard_map/all_to_all | solution.py:29
  80.0 1.0 copy-start.1
  82.6 12.0 %all-to-all-start.1 = ((bf16[2,65,32]{1,0,2:T(2,128)(2,1)}), bf16[2,65,32]{1,0,2:T(2,128)(2,1)S(1)}, u32[]{:S(2)}, u32[]{:S(2)}) async-start(bf16[2,65,32]{1,0,2:T(2,128)(2,1)} %copy.19), calls=%async_computation.1 | async-start | bytes 32768 | tf_op jit(solution)/shard_map/all_to_all | solution.py:33
where the time goes:
time: 125 us
  waiting for transfers between devices  41.6 us (33%)
  blocking collectives  24.6 us (20%)
  local copies, waits for them, and re-layouts  21.5 us (17%)
  starting transfers between devices  14.2 us (11%)
  matrix products  13.1 us (10%)
  other arithmetic  9.93 us (8%)
    all_to_all x1, waiting for transfers between devices, per_device(): lax.all_to_all(visibilities, 'ma', split_axis=1, concat_axis=2, tiled=True)  41.6 us
    psum x1, blocking collectives, per_device(): totals = lax.psum(partial_value, 'bl')  24.6 us
    unnamed x14, local copies, waits for them, and re-layouts  16.9 us
    all_to_all x1, starting transfers between devices, per_device(): lax.all_to_all(visibilities, 'ma', split_axis=1, concat_axis=2, tiled=True)  9.79 us
    dot_general x1, matrix products, per_device(): jnp.dot(one_hot, jnp.transpose(feed_gains), precision=lax.Precision.HIGHE...  7.6 us
    convert_element_type x1, other arithmetic, dft_weights(): sin_part = (jnp.sin(phases) * scale).astype(jnp.bfloat16)  5.22 us
    dot_general x1, matrix products, per_device(): jnp.einsum('mkc,mcl->kml', vectors, flat_blocks, preferred_element_type=j...  4.63 us
    all_to_all x1, starting transfers between devices, per_device(): lax.all_to_all(spectra_all, 'ma', split_axis=2, concat_axis=1, tiled=True)  4.41 us
  transfers between devices with their start and end apart: 2, of which 1 were waited for; matrix products, arithmetic and copies ran while one was open for 14% of the time, Pallas kernels for 0%

commit v1 on v0

--- a/solution.py
+++ b/solution.py
@@ -2,6 +2,7 @@
 import jax.numpy as jnp
 from jax import lax
 from jax.sharding import PartitionSpec as P
+from jax.lax import all_gather
 
 NT = 8192
 
@@ -62,7 +63,7 @@
     partial_value = jnp.einsum(
         "mkc,mcl->kml", vectors, flat_blocks, preferred_element_type=jnp.float32
     )
-    totals = lax.psum(partial_value, "bl")
+    totals = all_gather(partial_value, "bl").sum(axis=0)
     share_width = width // lax.axis_size("bl")
     result = lax.dynamic_slice_in_dim(totals, lax.axis_index("bl") * share_width, share_width, 2)
     return result

time: 125 us -> 136 us (1.088)
  blocking collectives: 24.6 us -> 34.6 us
    all_gather x0 -> x1, blocking collectives: none -> 34.6 us  [per_device(): totals = all_gather(partial_value, 'bl').sum(axis=0)]
    psum x1 -> x0, blocking collectives: 24.6 us -> none  [per_device(): totals = lax.psum(partial_value, 'bl')]
  transfers between devices with their start and end apart: 2 -> 2, of which waited for: 1 -> 1; matrix products, arithmetic and copies ran while one was open for 14% -> 13% of each run, Pallas kernels for 0% -> 0%
where the time goes in v1:
time: 136 us; the launch traced here: 135 us
  waiting for transfers between devices  41.6 us (31%)
  blocking collectives  34.6 us (25%)
  local copies, waits for them, and re-layouts  21.5 us (16%)
  starting transfers between devices  14.2 us (10%)
  matrix products  13.1 us (10%)
  other arithmetic  10.1 us (7%)
    all_to_all x1, waiting for transfers between devices, per_device(): lax.all_to_all(visibilities, 'ma', split_axis=1, concat_axis=2, tiled=True)  41.6 us
    all_gather x1, blocking collectives, per_device(): totals = all_gather(partial_value, 'bl').sum(axis=0)  34.6 us
    unnamed x14, local copies, waits for them, and re-layouts  16.9 us
    all_to_all x1, starting transfers between devices, per_device(): lax.all_to_all(visibilities, 'ma', split_axis=1, concat_axis=2, tiled=True)  9.79 us
    dot_general x1, matrix products, per_device(): jnp.dot(one_hot, jnp.transpose(feed_gains), precision=lax.Precision.HIGHE...  7.6 us
    convert_element_type x1, other arithmetic, dft_weights(): sin_part = (jnp.sin(phases) * scale).astype(jnp.bfloat16)  5.23 us
    dot_general x1, matrix products, per_device(): jnp.einsum('mkc,mcl->kml', vectors, flat_blocks, preferred_element_type=j...  4.63 us
    all_to_all x1, starting transfers between devices, per_device(): lax.all_to_all(spectra_all, 'ma', split_axis=2, concat_axis=1, tiled=True)  4.41 us
  transfers between devices with their start and end apart: 2, of which 1 were waited for; matrix products, arithmetic and copies ran while one was open for 13% of the time, Pallas kernels for 0%

profile of v1, /device:TPU:32, one launch (start us, length us, event | category | flops | bytes accessed | tf_op | source)
XLA Modules:
  0.0 135.3 jit_solution(5022039989409047522)
XLA Ops:
  0.0 0.0 copy-start
  0.0 14.5 %copy.14 = bf16[2,2080,256]{2,0,1:T(2,128)(2,1)} copy(bf16[2,2080,256]{2,1,0:T(8,128)(2,1)} %param.5) | data formatting | bytes 4259840 | tf_op args[0]
  14.5 9.8 %all-to-all-start = ((bf16[2,2080,256]{2,0,1:T(2,128)(2,1)}), bf16[2,2080,256]{2,0,1:T(2,128)(2,1)S(1)}, u32[]{:S(2)}, u32[]{:S(2)}) async-start(bf16[2,2080,256]{2,0,1:T(2,128)(2,1)} %copy.14), calls=%async_computation | async-start | bytes 4259840 | tf_op jit(solution)/shard_map/all_to_all | solution.py:30
  24.3 0.0 copy-done.2
  24.4 0.1 pad_add_fusion
  24.4 0.0 copy-done.3
  24.4 4.2 %fusion.24 = bf16[8192,32]{0,1:T(8,128)(2,1)S(1)} fusion(s32[32]{0:T(128)S(1)} %broadcast_add_fusion), kind=kLoop, calls=%fused_computation.29 | loop fusion | flops 4980736 | bytes 524416 | tf_op jit(solution)/shard_map/neg | solution.py:16
  28.7 5.2 %multiply_convert_fusion = (bf16[8192,32]{0,1:T(8,128)(2,1)S(1)}, bf16[8192,32]{0,1:T(8,128)(2,1)}) fusion(s32[32]{0:T(128)S(1)} %broadcast_add_fusion), kind=kLoop, calls=%fused_computation.24 | loop fusion | flops 4718592 | bytes 1048704 | tf_op jit(solution)/shard_map/convert_element_type | solution.py:15
  33.9 41.6 %all-to-all-done = bf16[2,2080,256]{2,0,1:T(2,128)(2,1)S(1)} async-done(((bf16[2,2080,256]{2,0,1:T(2,128)(2,1)}), bf16[2,2080,256]{2,0,1:T(2,128)(2,1)S(1)}, u32[]{:S(2)}, u32[]{:S(2)}) %all-to-all-start) | async-done | bytes 2129952 | tf_op jit(solution)/shard_map/all_to_all | solution.py:30
  75.5 3.0 %fusion.31 = (bf16[1,65,32,256]{3,0,1,2:T(2,128)(2,1)S(1)}, bf16[1,65,32,256]{3,0,1,2:T(2,128)(2,1)S(1)}) fusion(bf16[2,65,32,256]{3,0,1,2:T(2,128)(2,1)S(1)} %bitcast.38), kind=kLoop, calls=%fused_computation.53 | loop fusion | bytes 4259840 | tf_op jit(solution)/shard_map/slice | solution.py:22
  78.5 0.6 copy_bitcast_fusion
  79.1 0.1 pad.16
  79.2 0.7 copy.21
  80.0 0.0 copy-start.1
  80.0 0.1 pad.17
  80.1 0.7 copy.22
  80.8 0.2 copy-done.1
  81.0 0.9 fusion.13
  82.0 0.6 copy.17
  82.6 4.4 %all-to-all-start.1 = ((bf16[2,65,32]{1,0,2:T(2,128)(2,1)}), bf16[2,65,32]{1,0,2:T(2,128)(2,1)S(1)}, u32[]{:S(2)}, u32[]{:S(2)}) async-start(bf16[2,65,32]{1,0,2:T(2,128)(2,1)} %copy.17), calls=%async_computation.1 | async-start | bytes 32768 | tf_op jit(solution)/shard_map/all_to_all | solution.py:34
  87.0 7.6 %fusion = f32[4160,2]{0,1:T(2,128)S(1)} fusion(f32[2,1024]{1,0:T(2,128)S(1)} %copy-done, s32[4160]{0:T(1024)S(1)} %pad_add_fusion), kind=kOutput, calls=%fused_computation.1 | convolution fusion | flops 106496000 | bytes 58112 | tf_op jit(solution)/shard_map/dot_general | solution.py:40
  94.6 0.0 all-to-all-done.1
  94.6 0.1 fusion.28
  94.7 0.1 reshape.65
  94.8 0.1 reshape.66
  94.9 0.1 add_convert_fusion
  95.1 0.1 maximum_bitcast_fusion
  95.2 0.1 pad_maximum_fusion
  95.2 4.6 %convolution_bitcast_fusion = f32[2,1,1000]{2,0,1:T(2,128)S(1)} fusion(bf16[4160,1000]{1,0:T(8,128)(2,1)} %bitcast.37, bf16[2,4160,1]{1,2,0:T(2,128)(2,1)S(1)} %pad_maximum_fusion), kind=kOutput, calls=%fused_computation.18 | convolution fusion | flops 16640000 | bytes 8344640 | tf_op jit(solution)/shard_map/mkc,mcl->kml/dot_general | solution.py:63
  99.9 34.6 %all-gather = f32[16,1,1000]{2,1,0:T(1,128)S(1)} all-gather(f32[2,1,1000]{2,1,0:T(1,128)S(1)} %copy.18), channel_id=2, replica_groups=mesh['ma'=32,'bl'=8] {'bl'}, dimensions={0}, use_global_device_ids=true | all-gather | bytes 72000 | tf_op jit(solution)/shard_map/all_gather | solution.py:66
  134.5 0.2 reduce.6
  134.7 0.6 constant_dynamic-slice_fusion
  (11 shorter events, 0.2 us)
Async XLA Ops:
  0.0 87.0 %copy-start = (f32[2,1024]{1,0:T(2,128)S(1)}, f32[2,1024]{1,0:T(2,128)}, u32[]{:S(2)}) copy-start(f32[2,1024]{1,0:T(2,128)} %param.8) | copy-start | bytes 24580
  14.5 9.8 %copy-start.2 = (s32[2080,2]{0,1:T(2,128)S(1)}, s32[2080,2]{0,1:T(2,128)}, u32[]{:S(2)}) copy-start(s32[2080,2]{0,1:T(2,128)} %param.7) | copy-start | bytes 49924
  14.5 9.9 %copy-start.3 = (s32[32]{0:T(128)S(1)}, s32[32]{0:T(128)}, u32[]{:S(2)}) copy-start(s32[32]{0:T(128)} %param.9) | copy-start | bytes 388
  14.5 61.0 %all-to-all-start = ((bf16[2,2080,256]{2,0,1:T(2,128)(2,1)}), bf16[2,2080,256]{2,0,1:T(2,128)(2,1)S(1)}, u32[]{:S(2)}, u32[]{:S(2)}) async-start(bf16[2,2080,256]{2,0,1:T(2,128)(2,1)} %copy.14), calls=%async_computation | async-start | bytes 4259840 | tf_op jit(solution)/shard_map/all_to_all | solution.py:30
  80.0 1.0 copy-start.1
  82.6 12.0 %all-to-all-start.1 = ((bf16[2,65,32]{1,0,2:T(2,128)(2,1)}), bf16[2,65,32]{1,0,2:T(2,128)(2,1)S(1)}, u32[]{:S(2)}, u32[]{:S(2)}) async-start(bf16[2,65,32]{1,0,2:T(2,128)(2,1)} %copy.17), calls=%async_computation.1 | async-start | bytes 32768 | tf_op jit(solution)/shard_map/all_to_all | solution.py:34
